TPU v7x, 32 devices: a whole 2x2x4 slice. The times are simulated.
32 devices in a mesh: sub: 8 (over y, x, core), front: 4 (over z).
Axes of the slice: x: 2, y: 2, z: 4, core: 2. Of those that a mesh axis runs over, the one named last changes fastest.
Arguments:
- front_inverse: bfloat16 [8, 8192, 2048], P('sub', 'front'), may hold values from -0.75 to 0.75
- coupling: bfloat16 [8, 8192, 2048], P('sub', 'front'), may hold values from -0.0234375 to 0.0234375
- free_modes: bfloat16 [8, 300, 8192], P('sub', None, 'front'), may hold values from -0.125 to 0.125
- dof_offset: int32 [8, 256], P('sub', 'front'), may hold values from 0 to 2047, as said below
- interface_id: int32 [8, 256], replicated, may hold values from 0 to 1023, as said below
Outputs:
- attachment: bfloat16 [8, 256, 8192], P('sub', None, 'front')
- flexibility: float32 [1024, 1024], P(('sub', 'front'))
Inputs may be any that keep to these rules, and one draw needn't show every extreme that they name: `dof_offset`: within one substructure and one front the 64 offsets are distinct, and 0 and 2047 occur among them. `interface_id`: every value occurs exactly twice in the whole array.
All inputs are finite; a program needn't handle non-finite values.
Results may differ from a plain program's by a relative error of at most 0.02.
Values may be sent and summed in bfloat16 or wider, within the bound.
No kernel may reach another device: no remote copies, remote signals or barrier semaphores. Data moves between devices by JAX's collectives and lax.ppermute only.
A program may use at most 128 MiB of HBM per device.

v0:
```python
import jax
import jax.numpy as jnp
from jax import lax
from jax.sharding import PartitionSpec as P


def shifted(value, axis, steps):
    count = lax.axis_size(axis)
    leading, last = (max(0, -steps), min(count, count - steps))
    return lax.ppermute(value, axis, [(source, source + steps) for source in range(leading, last)])


def contract_last(left, right):
    return lax.dot_general(
        left, right, (((1,), (1,)), ((), ())), preferred_element_type=jnp.float32
    )


def on_device(front_inverse, coupling, free_modes, dof_offset, interface_id):
    inverse_block = front_inverse[0]
    coupling_block = coupling[0]
    mode_block = free_modes[0]
    offsets = dof_offset[0]
    order = inverse_block.shape[0]
    columns_all = interface_id.shape[1]
    per_front = offsets.shape[0]
    fronts = lax.axis_size("front")
    front_pos = lax.axis_index("front")
    sub_pos = lax.axis_index("sub")
    column_ids = jnp.arange(columns_all, dtype=jnp.int32)
    local_ids = jnp.arange(per_front, dtype=jnp.int32)
    row_ids = jnp.arange(order, dtype=jnp.int32)
    column_pick = (column_ids[:, None] == front_pos * per_front + local_ids[None, :]).astype(
        jnp.float32
    )
    row_pick = (offsets[:, None] == row_ids[None, :]).astype(jnp.float32)
    forces = jnp.dot(column_pick, row_pick, precision=lax.Precision.HIGHEST)
    groups = 1
    width = columns_all // groups
    force_groups = forces.reshape(groups, width, order)
    moments = groups + fronts - 1

    def forward(moment, carry):
        solved, outgoing = carry
        incoming = shifted(outgoing, "front", 1)
        panel = moment - front_pos
        valid = (panel >= 0) & (panel < groups)
        clipped = jnp.clip(panel, 0, groups - 1)

        def forward_active(unused):
            load = lax.dynamic_index_in_dim(force_groups, clipped, 0, keepdims=False)
            reduced = (load - contract_last(incoming, coupling_block)).astype(jnp.bfloat16)
            return contract_last(reduced, inverse_block).astype(jnp.bfloat16)

        def forward_waiting(unused):
            return outgoing

        result = lax.cond(valid, forward_active, forward_waiting, 0)
        solved = lax.dynamic_update_index_in_dim(solved, result, clipped, 0)
        return (solved, result)

    forward_start = (
        jnp.zeros((groups, width, order), jnp.bfloat16),
        jnp.zeros((width, order), jnp.bfloat16),
    )
    solved, forward_last = lax.fori_loop(0, moments, forward, forward_start)

    def backward(moment, carry):
        moved, outgoing = carry
        incoming = shifted(outgoing, "front", -1)
        panel = moment - (fronts - 1 - front_pos)
        valid = (panel >= 0) & (panel < groups)
        clipped = jnp.clip(panel, 0, groups - 1)

        def backward_active(unused):
            upper = lax.dynamic_index_in_dim(solved, clipped, 0, keepdims=False).astype(jnp.float32)
            reduced = (upper - incoming.astype(jnp.float32)).astype(jnp.bfloat16)
            displaced = jnp.dot(reduced, inverse_block, preferred_element_type=jnp.float32)
            handed = jnp.dot(
                displaced.astype(jnp.bfloat16), coupling_block, preferred_element_type=jnp.float32
            )
            return (displaced, handed.astype(jnp.bfloat16))

        def backward_waiting(unused):
            return (lax.dynamic_index_in_dim(moved, clipped, 0, keepdims=False), outgoing)

        displaced, handed = lax.cond(valid, backward_active, backward_waiting, 0)
        moved = lax.dynamic_update_index_in_dim(moved, displaced, clipped, 0)
        return (moved, handed)

    backward_start = (
        jnp.zeros((groups, width, order), jnp.float32),
        jnp.zeros((width, order), jnp.bfloat16),
    )
    moved, backward_last = lax.fori_loop(0, moments, backward, backward_start)
    displacement = moved.reshape(columns_all, order)
    modal = lax.psum(
        contract_last(displacement.astype(jnp.bfloat16), mode_block).astype(jnp.bfloat16), "front"
    )
    deflated = displacement - jnp.dot(modal, mode_block, preferred_element_type=jnp.float32)
    own_rows = jnp.take(deflated, offsets, axis=1).T
    total_ids = interface_id.shape[0] * columns_all // 2
    dual_ids = jnp.arange(total_ids, dtype=jnp.int32)
    owners = lax.axis_size("sub") * fronts
    share = total_ids // owners
    gathered = lax.all_gather(
        own_rows.astype(jnp.bfloat16), ("sub", "front"), axis=0, tiled=True
    ).astype(own_rows.dtype)
    subs_all = interface_id.shape[0]
    flat_labels = interface_id.reshape(-1)
    owner_pos = sub_pos * fronts + front_pos
    targets = owner_pos * share + jnp.arange(share, dtype=jnp.int32)
    row_select = (targets[:, None] == flat_labels[None, :]).astype(jnp.float32)
    reduced = jnp.einsum(
        "asc,scd->asd",
        row_select.reshape(share, subs_all, columns_all),
        gathered.reshape(subs_all, columns_all, columns_all),
        precision=lax.Precision.HIGHEST,
    )
    column_place = (flat_labels[:, None] == dual_ids[None, :]).astype(jnp.float32)
    flexibility = jnp.dot(
        reduced.reshape(share, subs_all * columns_all),
        column_place,
        precision=lax.Precision.HIGHEST,
    )
    return (deflated.astype(jnp.bfloat16)[None], flexibility)


def solution(mesh):
    return jax.shard_map(
        on_device,
        mesh=mesh,
        in_specs=(
            P("sub", "front", None),
            P("sub", "front", None),
            P("sub", None, "front"),
            P("sub", "front"),
            P(),
        ),
        out_specs=(P("sub", None, "front"), P(("sub", "front"), None)),
        check_vma=False,
    )
```

profile of v0, /device:TPU:0, one launch (start us, length us, event | category | flops | bytes accessed | tf_op | source)
XLA Modules:
  0.0 390.6 jit_solution(3004368580467127556)
XLA Ops:
  7.3 2.6 convolution_bitcast_fusion
  9.8 0.1 broadcast.48.clone
  9.9 126.6 %while.35 = (s32[]{:T(128)}, bf16[1,256,2048]{2,1,0:T(8,128)(2,1)}, bf16[256,2048]{1,0:T(8,128)(2,1)S(1)}, s32[]{:T(128)}, f32[1,256,2048]{2,1,0:T(8,128)}, /*in...) while((s32[]{:T(128)}, bf16[1,256,2048]{2,1,0:T(8,128)(2,1)}, ...), condition=%wide.region_3.4_spmd, body=%wide.region_0.3_spmd.sunk | while | flops 4296540160 | bytes 33554672 | solution.py:66
  10.0 0.1 copy.23
  10.1 5.0 %collective-permute-start = (bf16[256,2048]{1,0:T(8,128)(2,1)S(1)}, bf16[256,2048]{1,0:T(8,128)(2,1)S(1)}, u32[]{:S(2)}, u32[]{:S(2)}) collective-permute-start(bf16[256,2048]{1,0:T(8,128)(2,1)S(1)} %copy.23), channel_id=1, source_target_pairs={{0,1},{1,2},{2,3},{4,5},{5,6},{6,7},{8,9},{9,10},{10,11},{12,13},{... | collective-permute-start | bytes 3145736 | tf_op jit(solution)/shard_map/while/body/eval_jaxpr/ppermute | solution.py:10
  15.1 22.3 %collective-permute-done = bf16[256,2048]{1,0:T(8,128)(2,1)S(1)} collective-permute-done((bf16[256,2048]{1,0:T(8,128)(2,1)S(1)}, bf16[256,2048]{1,0:T(8,128)(2,1)S(1)}, u32[]{:S(2)}, u32[]{:S(2)}) %collective-permute-start) | collective-permute-done | bytes 1048608 | tf_op jit(solution)/shard_map/while/body/eval_jaxpr/ppermute | solution.py:10
  37.4 10.9 %conditional.4 = (bf16[256,2048]{1,0:T(8,128)(2,1)S(1)}) conditional(s32[]{:T(128)} %convert_element_type.98, bf16[256,2048]{1,0:T(8,128)(2,1)S(1)} %copy.23, (f32[1,256,2048]{2,1,0:T(8,128)}, bf16[256,2048]{1,0:T(8,128)(2,1)S(1)}, bf16[2048,2048]{1,0:T(8,128)(2,1)}, bf16[2048,2048]{1,0:T(8,128)(2,1)}) %tuple.101), branch_computations={%region_1.1_spmd, %region_2.2_spmd} | conditional | flops 4296540160 | bytes 20971528 | solution.py:58
  37.4 10.9 %convolution_convert_fusion = bf16[256,2048]{1,0:T(8,128)(2,1)S(1)} fusion(bf16[2048,2048]{1,0:T(8,128)(2,1)} %get-tuple-element.340, bf16[256,2048]{1,0:T(8,128)(2,1)S(1)} %get-tuple-element.338, bf16[2048,2048]{1,0:T(8,128)(2,1)} %get-tuple-element.339, f32[1,256,2048]{2,1,0:T(8,128)} %get-tuple-element.337), kind=kOutput, calls=%fused_computation.3 | convolution fusion | flops 4296540160 | bytes 20971520 | tf_op jit(solution)/shard_map/while/body/eval_jaxpr/cond/branch_1_fun/dot_general | solution.py:14
  48.4 0.1 copy.26
  48.5 0.9 copy-done.1
  49.3 0.1 copy.23
  49.4 1.4 collective-permute-start
  50.8 21.8 %collective-permute-done = bf16[256,2048]{1,0:T(8,128)(2,1)S(1)} collective-permute-done((bf16[256,2048]{1,0:T(8,128)(2,1)S(1)}, bf16[256,2048]{1,0:T(8,128)(2,1)S(1)}, u32[]{:S(2)}, u32[]{:S(2)}) %collective-permute-start) | collective-permute-done | bytes 1048608 | tf_op jit(solution)/shard_map/while/body/eval_jaxpr/ppermute | solution.py:10
  72.6 0.1 copy.26
  72.7 0.9 copy-done.1
  73.5 0.1 copy.23
  73.6 15.4 %collective-permute-start = (bf16[256,2048]{1,0:T(8,128)(2,1)S(1)}, bf16[256,2048]{1,0:T(8,128)(2,1)S(1)}, u32[]{:S(2)}, u32[]{:S(2)}) collective-permute-start(bf16[256,2048]{1,0:T(8,128)(2,1)S(1)} %copy.23), channel_id=1, source_target_pairs={{0,1},{1,2},{2,3},{4,5},{5,6},{6,7},{8,9},{9,10},{10,11},{12,13},{... | collective-permute-start | bytes 3145736 | tf_op jit(solution)/shard_map/while/body/eval_jaxpr/ppermute | solution.py:10
  89.1 20.9 %collective-permute-done = bf16[256,2048]{1,0:T(8,128)(2,1)S(1)} collective-permute-done((bf16[256,2048]{1,0:T(8,128)(2,1)S(1)}, bf16[256,2048]{1,0:T(8,128)(2,1)S(1)}, u32[]{:S(2)}, u32[]{:S(2)}) %collective-permute-start) | collective-permute-done | bytes 1048608 | tf_op jit(solution)/shard_map/while/body/eval_jaxpr/ppermute | solution.py:10
  110.0 0.1 copy.26
  110.1 0.9 copy-done.1
  110.9 0.1 copy.23
  111.0 4.5 %collective-permute-start = (bf16[256,2048]{1,0:T(8,128)(2,1)S(1)}, bf16[256,2048]{1,0:T(8,128)(2,1)S(1)}, u32[]{:S(2)}, u32[]{:S(2)}) collective-permute-start(bf16[256,2048]{1,0:T(8,128)(2,1)S(1)} %copy.23), channel_id=1, source_target_pairs={{0,1},{1,2},{2,3},{4,5},{5,6},{6,7},{8,9},{9,10},{10,11},{12,13},{... | collective-permute-start | bytes 3145736 | tf_op jit(solution)/shard_map/while/body/eval_jaxpr/ppermute | solution.py:10
  115.5 20.0 %collective-permute-done = bf16[256,2048]{1,0:T(8,128)(2,1)S(1)} collective-permute-done((bf16[256,2048]{1,0:T(8,128)(2,1)S(1)}, bf16[256,2048]{1,0:T(8,128)(2,1)S(1)}, u32[]{:S(2)}, u32[]{:S(2)}) %collective-permute-start) | collective-permute-done | bytes 1048608 | tf_op jit(solution)/shard_map/while/body/eval_jaxpr/ppermute | solution.py:10
  135.6 0.9 copy-done.1
  136.5 1.6 broadcast_in_dim.49
  138.1 0.1 broadcast.48
  138.2 144.6 %while.36 = (s32[]{:T(128)}, f32[1,256,2048]{2,1,0:T(8,128)}, bf16[256,2048]{1,0:T(8,128)(2,1)S(1)}, s32[]{:T(128)}, bf16[1,256,2048]{2,1,0:T(8,128)(2,1)S(1)}, ...) while((s32[]{:T(128)}, f32[1,256,2048]{2,1,0:T(8,128)}, ...), condition=%wide.region_7.8_spmd, body=%wide.region_4.7_spmd.sunk | while | flops 4298113024 | bytes 70254888 | solution.py:95
  138.2 1.3 collective-permute-start.1
  139.5 32.5 %collective-permute-done.1 = bf16[256,2048]{1,0:T(8,128)(2,1)} collective-permute-done((bf16[256,2048]{1,0:T(8,128)(2,1)S(1)}, bf16[256,2048]{1,0:T(8,128)(2,1)}, u32[]{:S(2)}, u32[]{:S(2)}) %collective-permute-start.1) | collective-permute-done | bytes 1048608 | tf_op jit(solution)/shard_map/while/body/eval_jaxpr/ppermute | solution.py:10
  172.1 1.3 collective-permute-start.1
  173.4 22.9 %collective-permute-done.1 = bf16[256,2048]{1,0:T(8,128)(2,1)} collective-permute-done((bf16[256,2048]{1,0:T(8,128)(2,1)S(1)}, bf16[256,2048]{1,0:T(8,128)(2,1)}, u32[]{:S(2)}, u32[]{:S(2)}) %collective-permute-start.1) | collective-permute-done | bytes 1048608 | tf_op jit(solution)/shard_map/while/body/eval_jaxpr/ppermute | solution.py:10
  196.3 1.3 collective-permute-start.1
  197.5 31.3 %collective-permute-done.1 = bf16[256,2048]{1,0:T(8,128)(2,1)} collective-permute-done((bf16[256,2048]{1,0:T(8,128)(2,1)S(1)}, bf16[256,2048]{1,0:T(8,128)(2,1)}, u32[]{:S(2)}, u32[]{:S(2)}) %collective-permute-start.1) | collective-permute-done | bytes 1048608 | tf_op jit(solution)/shard_map/while/body/eval_jaxpr/ppermute | solution.py:10
  228.8 1.3 collective-permute-start.1
  230.1 44.1 %collective-permute-done.1 = bf16[256,2048]{1,0:T(8,128)(2,1)} collective-permute-done((bf16[256,2048]{1,0:T(8,128)(2,1)S(1)}, bf16[256,2048]{1,0:T(8,128)(2,1)}, u32[]{:S(2)}, u32[]{:S(2)}) %collective-permute-start.1) | collective-permute-done | bytes 1048608 | tf_op jit(solution)/shard_map/while/body/eval_jaxpr/ppermute | solution.py:10
  274.2 8.5 %conditional.5 = ((bf16[256,2048]{1,0:T(8,128)(2,1)S(1)}, f32[1,256,2048]{2,1,0:T(8,128)})) conditional(s32[]{:T(128)} %convert_element_type.99, (bf16[256,2048]{1,0:T(8,128)(2,1)S(1)}, f32[1,256,2048]{2,1,0:T(8,128)}) %tuple.103, (bf16[1,256,2048]{2,1,0:T(8,128)(2,1)S(1)}, bf16[256,2048]{1,0:T(8,128)(2,1)}, bf16[2048,2048]{1,0:T(8,128)(2,1)}, ...), branch_computations={%region_5.5_spmd, %region_6.6_spmd} | conditional | flops 4298113024 | bytes 66060368 | solution.py:87
  274.2 6.2 %fusion.2 = f32[256,2048]{1,0:T(8,128)S(1)} fusion(bf16[2048,2048]{1,0:T(8,128)(2,1)} %get-tuple-element.350, bf16[256,2048]{1,0:T(8,128)(2,1)} %get-tuple-element.349, bf16[1,256,2048]{2,1,0:T(8,128)(2,1)S(1)} %get-tuple-element.348), kind=kOutput, calls=%fused_computation.7 | convolution fusion | flops 2149580800 | bytes 12582912 | tf_op jit(solution)/shard_map/while/body/eval_jaxpr/cond/branch_1_fun/dot_general | solution.py:78
  280.4 2.3 convolution_convert_fusion.1
  282.8 3.1 fusion.11
  286.0 0.2 all-gather.2.cloned.1.call-start
  286.3 33.1 %all-reduce.2.cloned.1.call-done = bf16[256,300]{1,0:T(8,128)(2,1)} async-done(((bf16[256,300]{1,0:T(8,128)(2,1)}), bf16[256,300]{1,0:T(8,128)(2,1)}) %all-reduce.2.cloned.1.call-update) | async-done | bytes 153616 | tf_op jit(solution)/shard_map/psum | solution.py:97
  319.4 2.6 convolution_subtract_fusion.1
  322.0 1.5 copy.8
  323.5 0.7 gather_fusion
  324.2 0.7 select_convert_fusion
  324.9 53.6 %all-gather.2.cloned.1.call-done = bf16[2048,256]{1,0:T(8,128)(2,1)} async-done(((bf16[64,256]{1,0:T(8,128)(2,1)}), bf16[2048,256]{1,0:T(8,128)(2,1)}) %all-gather.2.cloned.1.call-update) | async-done | bytes 1048592 | tf_op jit(solution)/shard_map/all_gather | solution.py:106
  378.5 1.5 convolution_bitcast_fusion.1
  380.1 3.8 fusion.6
  (36 shorter events, 0.3 us)
Async XLA Ops:
  7.2 275.7 %copy-start = (bf16[1,300,2048]{2,1,0:T(8,128)(2,1)S(1)}, bf16[1,300,2048]{2,1,0:T(8,128)(2,1)}, u32[]{:S(2)}) copy-start(bf16[1,300,2048]{2,1,0:T(8,128)(2,1)} %param.15) | copy-start | bytes 3686404
  7.2 312.2 %all-reduce.2.cloned.1.call-start = ((), (), s32[]{:S(2)}) async-start(), calls=%async_computation | async-start | bytes 393216 | tf_op jit(solution)/shard_map/psum | solution.py:97
  10.1 27.4 %collective-permute-start = (bf16[256,2048]{1,0:T(8,128)(2,1)S(1)}, bf16[256,2048]{1,0:T(8,128)(2,1)S(1)}, u32[]{:S(2)}, u32[]{:S(2)}) collective-permute-start(bf16[256,2048]{1,0:T(8,128)(2,1)S(1)} %copy.23), channel_id=1, source_target_pairs={{0,1},{1,2},{2,3},{4,5},{5,6},{6,7},{8,9},{9,10},{10,11},{12,13},{... | collective-permute-start | bytes 3145736 | tf_op jit(solution)/shard_map/while/body/eval_jaxpr/ppermute | solution.py:10
  48.4 1.0 copy-start.1
  49.4 23.1 %collective-permute-start = (bf16[256,2048]{1,0:T(8,128)(2,1)S(1)}, bf16[256,2048]{1,0:T(8,128)(2,1)S(1)}, u32[]{:S(2)}, u32[]{:S(2)}) collective-permute-start(bf16[256,2048]{1,0:T(8,128)(2,1)S(1)} %copy.23), channel_id=1, source_target_pairs={{0,1},{1,2},{2,3},{4,5},{5,6},{6,7},{8,9},{9,10},{10,11},{12,13},{... | collective-permute-start | bytes 3145736 | tf_op jit(solution)/shard_map/while/body/eval_jaxpr/ppermute | solution.py:10
  72.6 1.0 copy-start.1
  73.6 36.3 %collective-permute-start = (bf16[256,2048]{1,0:T(8,128)(2,1)S(1)}, bf16[256,2048]{1,0:T(8,128)(2,1)S(1)}, u32[]{:S(2)}, u32[]{:S(2)}) collective-permute-start(bf16[256,2048]{1,0:T(8,128)(2,1)S(1)} %copy.23), channel_id=1, source_target_pairs={{0,1},{1,2},{2,3},{4,5},{5,6},{6,7},{8,9},{9,10},{10,11},{12,13},{... | collective-permute-start | bytes 3145736 | tf_op jit(solution)/shard_map/while/body/eval_jaxpr/ppermute | solution.py:10
  110.0 1.0 copy-start.1
  111.0 24.5 %collective-permute-start = (bf16[256,2048]{1,0:T(8,128)(2,1)S(1)}, bf16[256,2048]{1,0:T(8,128)(2,1)S(1)}, u32[]{:S(2)}, u32[]{:S(2)}) collective-permute-start(bf16[256,2048]{1,0:T(8,128)(2,1)S(1)} %copy.23), channel_id=1, source_target_pairs={{0,1},{1,2},{2,3},{4,5},{5,6},{6,7},{8,9},{9,10},{10,11},{12,13},{... | collective-permute-start | bytes 3145736 | tf_op jit(solution)/shard_map/while/body/eval_jaxpr/ppermute | solution.py:10
  135.5 1.0 copy-start.1
  136.5 1.7 copy-start.2
  138.2 33.8 %collective-permute-start.1 = (bf16[256,2048]{1,0:T(8,128)(2,1)S(1)}, bf16[256,2048]{1,0:T(8,128)(2,1)}, u32[]{:S(2)}, u32[]{:S(2)}) collective-permute-start(bf16[256,2048]{1,0:T(8,128)(2,1)S(1)} %get-tuple-element.526), channel_id=1, source_target_pairs={{1,0},{2,1},{3,2},{5,4},{6,5},{7,6},{9,8},{10,9},{11,10},{13,12},{... | collective-permute-start | bytes 3145736 | tf_op jit(solution)/shard_map/while/body/eval_jaxpr/ppermute | solution.py:10
  172.1 24.2 %collective-permute-start.1 = (bf16[256,2048]{1,0:T(8,128)(2,1)S(1)}, bf16[256,2048]{1,0:T(8,128)(2,1)}, u32[]{:S(2)}, u32[]{:S(2)}) collective-permute-start(bf16[256,2048]{1,0:T(8,128)(2,1)S(1)} %get-tuple-element.526), channel_id=1, source_target_pairs={{1,0},{2,1},{3,2},{5,4},{6,5},{7,6},{9,8},{10,9},{11,10},{13,12},{... | collective-permute-start | bytes 3145736 | tf_op jit(solution)/shard_map/while/body/eval_jaxpr/ppermute | solution.py:10
  196.3 32.6 %collective-permute-start.1 = (bf16[256,2048]{1,0:T(8,128)(2,1)S(1)}, bf16[256,2048]{1,0:T(8,128)(2,1)}, u32[]{:S(2)}, u32[]{:S(2)}) collective-permute-start(bf16[256,2048]{1,0:T(8,128)(2,1)S(1)} %get-tuple-element.526), channel_id=1, source_target_pairs={{1,0},{2,1},{3,2},{5,4},{6,5},{7,6},{9,8},{10,9},{11,10},{13,12},{... | collective-permute-start | bytes 3145736 | tf_op jit(solution)/shard_map/while/body/eval_jaxpr/ppermute | solution.py:10
  228.8 45.4 %collective-permute-start.1 = (bf16[256,2048]{1,0:T(8,128)(2,1)S(1)}, bf16[256,2048]{1,0:T(8,128)(2,1)}, u32[]{:S(2)}, u32[]{:S(2)}) collective-permute-start(bf16[256,2048]{1,0:T(8,128)(2,1)S(1)} %get-tuple-element.526), channel_id=1, source_target_pairs={{1,0},{2,1},{3,2},{5,4},{6,5},{7,6},{9,8},{10,9},{11,10},{13,12},{... | collective-permute-start | bytes 3145736 | tf_op jit(solution)/shard_map/while/body/eval_jaxpr/ppermute | solution.py:10
  274.2 6.2 %copy-start.7 = (bf16[2048,2048]{1,0:T(8,128)(2,1)S(1)}, bf16[2048,2048]{1,0:T(8,128)(2,1)}, u32[]{:S(2)}) copy-start(bf16[2048,2048]{1,0:T(8,128)(2,1)} %get-tuple-element.351) | copy-start | bytes 25165828 | tf_op jit(solution)/shard_map/while/body/eval_jaxpr/cond
  280.4 2.4 copy-start.3
  282.8 3.4 copy-start.6
  282.8 36.5 %copy-start.4 = (f32[1,256,2048]{2,1,0:T(8,128)S(1)}, f32[1,256,2048]{2,1,0:T(8,128)}, u32[]{:S(2)}) copy-start(f32[1,256,2048]{2,1,0:T(8,128)} %get-tuple-element.367) | copy-start | bytes 6291460
  286.0 92.5 %all-gather.2.cloned.1.call-start = ((), (), s32[]{:S(2)}) async-start(), calls=%async_computation.1 | async-start | bytes 1081344 | tf_op jit(solution)/shard_map/all_gather | solution.py:106
  322.0 2.9 copy-start.5
Sparse Core Ops, SparseCore 0:
  286.1 33.1 all-reduce.1
  325.0 53.4 all-gather.1
where the time goes:
time: 391 us
  waiting for transfers between devices  302 us (77%)
  matrix products  33 us (8%)
  starting transfers between devices  31.6 us (8%)
  between operations  14.2 us (4%)
  local copies, waits for them, and re-layouts  8.29 us (2%)
    ppermute x8, waiting for transfers between devices, shifted(): lax.ppermute(value, axis, [(source, source + steps) for source in range(l...  216 us
    all_gather x1, waiting for transfers between devices, on_device(): lax.all_gather(own_rows.astype(jnp.bfloat16), ('sub', 'front'), axis=0, t...  53.6 us
    psum x1, waiting for transfers between devices, on_device(): lax.psum(contract_last(displacement.astype(jnp.bfloat16), mode_block).ast...  33.1 us
    ppermute x8, starting transfers between devices, shifted(): lax.ppermute(value, axis, [(source, source + steps) for source in range(l...  31.4 us
    dot_general x2, matrix products, contract_last(): lax.dot_general(left, right, (((1,), (1,)), ((), ())), preferred_element_...  14.1 us
  transfers between devices with their start and end apart: 10, of which 10 were waited for; matrix products, arithmetic and copies ran while one was open for 0% of the time, Pallas kernels for 0%

commit v1 on v0

--- a/solution.py
+++ b/solution.py
@@ -94,8 +94,12 @@
     )
     moved, backward_last = lax.fori_loop(0, moments, backward, backward_start)
     displacement = moved.reshape(columns_all, order)
-    modal = lax.psum(
-        contract_last(displacement.astype(jnp.bfloat16), mode_block).astype(jnp.bfloat16), "front"
+    modal = jnp.sum(
+        lax.all_gather(
+            contract_last(displacement.astype(jnp.bfloat16), mode_block).astype(jnp.bfloat16),
+            "front",
+        ),
+        axis=0,
     )
     deflated = displacement - jnp.dot(modal, mode_block, preferred_element_type=jnp.float32)
     own_rows = jnp.take(deflated, offsets, axis=1).T

time: 391 us -> 377 us (0.964)
  waiting for transfers between devices: 302 us -> 268 us
  blocking collectives: 0 us -> 17 us
    psum x1 -> x0, waiting for transfers between devices: 33.1 us -> none  [on_device(): lax.psum(contract_last(displacement.astype(jnp.bfloat16), mode_block).ast...]
    all_gather x0 -> x1, blocking collectives: none -> 17 us  [on_device(): lax.all_gather(contract_last(displacement.astype(jnp.bfloat16), mode_bloc...]
  transfers between devices with their start and end apart: 10 -> 9, of which waited for: 10 -> 9; matrix products, arithmetic and copies ran while one was open for 0% -> 0% of each run, Pallas kernels for 0% -> 0%
where the time goes in v1:
time: 377 us
  waiting for transfers between devices  268 us (71%)
  starting transfers between devices  31.4 us (8%)
  matrix products  31 us (8%)
  blocking collectives  17 us (5%)
  between operations  14.2 us (4%)
  local copies, waits for them, and re-layouts  10.7 us (3%)
  other arithmetic  3.94 us (1%)
    ppermute x8, waiting for transfers between devices, shifted(): lax.ppermute(value, axis, [(source, source + steps) for source in range(l...  216 us
    all_gather x1, waiting for transfers between devices, on_device(): lax.all_gather(own_rows.astype(jnp.bfloat16), ('sub', 'front'), axis=0, t...  52.5 us
    ppermute x8, starting transfers between devices, shifted(): lax.ppermute(value, axis, [(source, source + steps) for source in range(l...  31.4 us
    all_gather x1, blocking collectives, on_device(): lax.all_gather(contract_last(displacement.astype(jnp.bfloat16), mode_bloc...  17 us
    dot_general x2, matrix products, contract_last(): lax.dot_general(left, right, (((1,), (1,)), ((), ())), preferred_element_...  13 us
  transfers between devices with their start and end apart: 9, of which 9 were waited for; matrix products, arithmetic and copies ran while one was open for 0% of the time, Pallas kernels for 0%

profile of v1, /device:TPU:0, one launch (start us, length us, event | category | flops | bytes accessed | tf_op | source)
XLA Modules:
  0.0 376.8 jit_solution(15770255727446597788)
XLA Ops:
  7.2 0.7 fusion.21
  8.0 0.7 compare_and_fusion
  8.7 2.5 convolution_bitcast_fusion
  11.1 0.1 broadcast.48.clone
  11.3 126.5 %while.35 = (s32[]{:T(128)}, bf16[1,256,2048]{2,1,0:T(8,128)(2,1)}, bf16[256,2048]{1,0:T(8,128)(2,1)S(1)}, s32[]{:T(128)}, f32[1,256,2048]{2,1,0:T(8,128)}, /*in...) while((s32[]{:T(128)}, bf16[1,256,2048]{2,1,0:T(8,128)(2,1)}, ...), condition=%wide.region_3.4_spmd, body=%wide.region_0.3_spmd.sunk | while | flops 4296540160 | bytes 33554672 | solution.py:66
  11.3 0.1 copy.25
  11.4 5.0 %collective-permute-start = (bf16[256,2048]{1,0:T(8,128)(2,1)S(1)}, bf16[256,2048]{1,0:T(8,128)(2,1)S(1)}, u32[]{:S(2)}, u32[]{:S(2)}) collective-permute-start(bf16[256,2048]{1,0:T(8,128)(2,1)S(1)} %copy.25), channel_id=1, source_target_pairs={{0,1},{1,2},{2,3},{4,5},{5,6},{6,7},{8,9},{9,10},{10,11},{12,13},{... | collective-permute-start | bytes 3145736 | tf_op jit(solution)/shard_map/while/body/eval_jaxpr/ppermute | solution.py:10
  16.4 22.3 %collective-permute-done = bf16[256,2048]{1,0:T(8,128)(2,1)S(1)} collective-permute-done((bf16[256,2048]{1,0:T(8,128)(2,1)S(1)}, bf16[256,2048]{1,0:T(8,128)(2,1)S(1)}, u32[]{:S(2)}, u32[]{:S(2)}) %collective-permute-start) | collective-permute-done | bytes 1048608 | tf_op jit(solution)/shard_map/while/body/eval_jaxpr/ppermute | solution.py:10
  38.7 10.9 %conditional.4 = (bf16[256,2048]{1,0:T(8,128)(2,1)S(1)}) conditional(s32[]{:T(128)} %convert_element_type.100, bf16[256,2048]{1,0:T(8,128)(2,1)S(1)} %copy.25, (f32[1,256,2048]{2,1,0:T(8,128)}, bf16[256,2048]{1,0:T(8,128)(2,1)S(1)}, bf16[2048,2048]{1,0:T(8,128)(2,1)}, bf16[2048,2048]{1,0:T(8,128)(2,1)}) %tuple.101), branch_computations={%region_1.1_spmd, %region_2.2_spmd} | conditional | flops 4296540160 | bytes 20971528 | solution.py:58
  38.7 10.9 %convolution_convert_fusion = bf16[256,2048]{1,0:T(8,128)(2,1)S(1)} fusion(bf16[2048,2048]{1,0:T(8,128)(2,1)} %get-tuple-element.340, bf16[256,2048]{1,0:T(8,128)(2,1)S(1)} %get-tuple-element.338, bf16[2048,2048]{1,0:T(8,128)(2,1)} %get-tuple-element.339, f32[1,256,2048]{2,1,0:T(8,128)} %get-tuple-element.337), kind=kOutput, calls=%fused_computation.3 | convolution fusion | flops 4296540160 | bytes 20971520 | tf_op jit(solution)/shard_map/while/body/eval_jaxpr/cond/branch_1_fun/dot_general | solution.py:14
  49.7 0.1 copy.28
  49.8 0.9 copy-done.1
  50.6 0.1 copy.25
  50.8 1.4 collective-permute-start
  52.1 21.7 %collective-permute-done = bf16[256,2048]{1,0:T(8,128)(2,1)S(1)} collective-permute-done((bf16[256,2048]{1,0:T(8,128)(2,1)S(1)}, bf16[256,2048]{1,0:T(8,128)(2,1)S(1)}, u32[]{:S(2)}, u32[]{:S(2)}) %collective-permute-start) | collective-permute-done | bytes 1048608 | tf_op jit(solution)/shard_map/while/body/eval_jaxpr/ppermute | solution.py:10
  73.9 0.1 copy.28
  74.0 0.9 copy-done.1
  74.9 15.4 %collective-permute-start = (bf16[256,2048]{1,0:T(8,128)(2,1)S(1)}, bf16[256,2048]{1,0:T(8,128)(2,1)S(1)}, u32[]{:S(2)}, u32[]{:S(2)}) collective-permute-start(bf16[256,2048]{1,0:T(8,128)(2,1)S(1)} %copy.25), channel_id=1, source_target_pairs={{0,1},{1,2},{2,3},{4,5},{5,6},{6,7},{8,9},{9,10},{10,11},{12,13},{... | collective-permute-start | bytes 3145736 | tf_op jit(solution)/shard_map/while/body/eval_jaxpr/ppermute | solution.py:10
  90.4 20.9 %collective-permute-done = bf16[256,2048]{1,0:T(8,128)(2,1)S(1)} collective-permute-done((bf16[256,2048]{1,0:T(8,128)(2,1)S(1)}, bf16[256,2048]{1,0:T(8,128)(2,1)S(1)}, u32[]{:S(2)}, u32[]{:S(2)}) %collective-permute-start) | collective-permute-done | bytes 1048608 | tf_op jit(solution)/shard_map/while/body/eval_jaxpr/ppermute | solution.py:10
  111.4 0.9 copy-done.1
  112.3 4.5 %collective-permute-start = (bf16[256,2048]{1,0:T(8,128)(2,1)S(1)}, bf16[256,2048]{1,0:T(8,128)(2,1)S(1)}, u32[]{:S(2)}, u32[]{:S(2)}) collective-permute-start(bf16[256,2048]{1,0:T(8,128)(2,1)S(1)} %copy.25), channel_id=1, source_target_pairs={{0,1},{1,2},{2,3},{4,5},{5,6},{6,7},{8,9},{9,10},{10,11},{12,13},{... | collective-permute-start | bytes 3145736 | tf_op jit(solution)/shard_map/while/body/eval_jaxpr/ppermute | solution.py:10
  116.8 20.0 %collective-permute-done = bf16[256,2048]{1,0:T(8,128)(2,1)S(1)} collective-permute-done((bf16[256,2048]{1,0:T(8,128)(2,1)S(1)}, bf16[256,2048]{1,0:T(8,128)(2,1)S(1)}, u32[]{:S(2)}, u32[]{:S(2)}) %collective-permute-start) | collective-permute-done | bytes 1048608 | tf_op jit(solution)/shard_map/while/body/eval_jaxpr/ppermute | solution.py:10
  136.9 0.9 copy-done.1
  137.8 1.6 broadcast_in_dim.49
  139.4 0.1 broadcast.48
  139.5 144.6 %while.36 = (s32[]{:T(128)}, f32[1,256,2048]{2,1,0:T(8,128)}, bf16[256,2048]{1,0:T(8,128)(2,1)S(1)}, s32[]{:T(128)}, bf16[1,256,2048]{2,1,0:T(8,128)(2,1)S(1)}, ...) while((s32[]{:T(128)}, f32[1,256,2048]{2,1,0:T(8,128)}, ...), condition=%wide.region_7.8_spmd, body=%wide.region_4.7_spmd.sunk | while | flops 4298113024 | bytes 70254888 | solution.py:95
  139.5 1.3 collective-permute-start.1
  140.8 32.5 %collective-permute-done.1 = bf16[256,2048]{1,0:T(8,128)(2,1)} collective-permute-done((bf16[256,2048]{1,0:T(8,128)(2,1)S(1)}, bf16[256,2048]{1,0:T(8,128)(2,1)}, u32[]{:S(2)}, u32[]{:S(2)}) %collective-permute-start.1) | collective-permute-done | bytes 1048608 | tf_op jit(solution)/shard_map/while/body/eval_jaxpr/ppermute | solution.py:10
  173.3 1.3 collective-permute-start.1
  174.6 22.9 %collective-permute-done.1 = bf16[256,2048]{1,0:T(8,128)(2,1)} collective-permute-done((bf16[256,2048]{1,0:T(8,128)(2,1)S(1)}, bf16[256,2048]{1,0:T(8,128)(2,1)}, u32[]{:S(2)}, u32[]{:S(2)}) %collective-permute-start.1) | collective-permute-done | bytes 1048608 | tf_op jit(solution)/shard_map/while/body/eval_jaxpr/ppermute | solution.py:10
  197.5 1.3 collective-permute-start.1
  198.8 31.3 %collective-permute-done.1 = bf16[256,2048]{1,0:T(8,128)(2,1)} collective-permute-done((bf16[256,2048]{1,0:T(8,128)(2,1)S(1)}, bf16[256,2048]{1,0:T(8,128)(2,1)}, u32[]{:S(2)}, u32[]{:S(2)}) %collective-permute-start.1) | collective-permute-done | bytes 1048608 | tf_op jit(solution)/shard_map/while/body/eval_jaxpr/ppermute | solution.py:10
  230.1 1.3 collective-permute-start.1
  231.4 44.1 %collective-permute-done.1 = bf16[256,2048]{1,0:T(8,128)(2,1)} collective-permute-done((bf16[256,2048]{1,0:T(8,128)(2,1)S(1)}, bf16[256,2048]{1,0:T(8,128)(2,1)}, u32[]{:S(2)}, u32[]{:S(2)}) %collective-permute-start.1) | collective-permute-done | bytes 1048608 | tf_op jit(solution)/shard_map/while/body/eval_jaxpr/ppermute | solution.py:10
  275.5 8.6 %conditional.5 = ((bf16[256,2048]{1,0:T(8,128)(2,1)S(1)}, f32[1,256,2048]{2,1,0:T(8,128)})) conditional(s32[]{:T(128)} %convert_element_type.101, (bf16[256,2048]{1,0:T(8,128)(2,1)S(1)}, f32[1,256,2048]{2,1,0:T(8,128)}) %tuple.103, (bf16[1,256,2048]{2,1,0:T(8,128)(2,1)S(1)}, bf16[256,2048]{1,0:T(8,128)(2,1)}, bf16[2048,2048]{1,0:T(8,128)(2,1)}, ...), branch_computations={%region_5.5_spmd, %region_6.6_spmd} | conditional | flops 4298113024 | bytes 66060368 | solution.py:87
  275.5 6.2 %fusion.2 = f32[256,2048]{1,0:T(8,128)S(1)} fusion(bf16[2048,2048]{1,0:T(8,128)(2,1)} %get-tuple-element.350, bf16[256,2048]{1,0:T(8,128)(2,1)} %get-tuple-element.349, bf16[1,256,2048]{2,1,0:T(8,128)(2,1)S(1)} %get-tuple-element.348), kind=kOutput, calls=%fused_computation.7 | convolution fusion | flops 2149580800 | bytes 12582912 | tf_op jit(solution)/shard_map/while/body/eval_jaxpr/cond/branch_1_fun/dot_general | solution.py:78
  281.7 2.3 convolution_convert_fusion.1
  284.1 2.1 fusion.11
  286.2 17.0 %all-gather = bf16[1024,300]{0,1:T(8,128)(2,1)} all-gather(bf16[256,300]{0,1:T(8,128)(2,1)S(1)} %fusion.11), channel_id=2, replica_groups=mesh['sub'=8,'front'=4] {'front'}, dimensions={0}, use_global_device_ids=true | all-gather | bytes 768000 | tf_op jit(solution)/shard_map/all_gather | solution.py:98
  303.2 2.4 reshape.90
  305.6 1.8 reduce_sum.12
  307.5 1.7 convolution_subtract_fusion.1
  309.2 1.5 copy.10
  310.7 0.7 gather_fusion
  311.4 0.7 select_convert_fusion
  312.2 52.5 %all-gather.3.cloned.1.call-done = bf16[2048,256]{1,0:T(8,128)(2,1)} async-done(((bf16[64,256]{1,0:T(8,128)(2,1)}), bf16[2048,256]{1,0:T(8,128)(2,1)}) %all-gather.3.cloned.1.call-update) | async-done | bytes 1048592 | tf_op jit(solution)/shard_map/all_gather | solution.py:110
  364.7 1.5 convolution_bitcast_fusion.1
  366.2 3.8 fusion.6
  (34 shorter events, 0.5 us)
Async XLA Ops:
  7.2 276.9 %copy-start = (bf16[1,300,2048]{2,1,0:T(8,128)(2,1)S(1)}, bf16[1,300,2048]{2,1,0:T(8,128)(2,1)}, u32[]{:S(2)}) copy-start(bf16[1,300,2048]{2,1,0:T(8,128)(2,1)} %param.15) | copy-start | bytes 3686404
  7.2 357.5 %all-gather.3.cloned.1.call-start = ((), (), s32[]{:S(2)}) async-start(), calls=%async_computation | async-start | bytes 1081344 | tf_op jit(solution)/shard_map/all_gather | solution.py:110
  11.4 27.4 %collective-permute-start = (bf16[256,2048]{1,0:T(8,128)(2,1)S(1)}, bf16[256,2048]{1,0:T(8,128)(2,1)S(1)}, u32[]{:S(2)}, u32[]{:S(2)}) collective-permute-start(bf16[256,2048]{1,0:T(8,128)(2,1)S(1)} %copy.25), channel_id=1, source_target_pairs={{0,1},{1,2},{2,3},{4,5},{5,6},{6,7},{8,9},{9,10},{10,11},{12,13},{... | collective-permute-start | bytes 3145736 | tf_op jit(solution)/shard_map/while/body/eval_jaxpr/ppermute | solution.py:10
  49.7 1.0 copy-start.1
  50.8 23.1 %collective-permute-start = (bf16[256,2048]{1,0:T(8,128)(2,1)S(1)}, bf16[256,2048]{1,0:T(8,128)(2,1)S(1)}, u32[]{:S(2)}, u32[]{:S(2)}) collective-permute-start(bf16[256,2048]{1,0:T(8,128)(2,1)S(1)} %copy.25), channel_id=1, source_target_pairs={{0,1},{1,2},{2,3},{4,5},{5,6},{6,7},{8,9},{9,10},{10,11},{12,13},{... | collective-permute-start | bytes 3145736 | tf_op jit(solution)/shard_map/while/body/eval_jaxpr/ppermute | solution.py:10
  73.9 1.0 copy-start.1
  74.9 36.3 %collective-permute-start = (bf16[256,2048]{1,0:T(8,128)(2,1)S(1)}, bf16[256,2048]{1,0:T(8,128)(2,1)S(1)}, u32[]{:S(2)}, u32[]{:S(2)}) collective-permute-start(bf16[256,2048]{1,0:T(8,128)(2,1)S(1)} %copy.25), channel_id=1, source_target_pairs={{0,1},{1,2},{2,3},{4,5},{5,6},{6,7},{8,9},{9,10},{10,11},{12,13},{... | collective-permute-start | bytes 3145736 | tf_op jit(solution)/shard_map/while/body/eval_jaxpr/ppermute | solution.py:10
  111.2 1.0 copy-start.1
  112.3 24.5 %collective-permute-start = (bf16[256,2048]{1,0:T(8,128)(2,1)S(1)}, bf16[256,2048]{1,0:T(8,128)(2,1)S(1)}, u32[]{:S(2)}, u32[]{:S(2)}) collective-permute-start(bf16[256,2048]{1,0:T(8,128)(2,1)S(1)} %copy.25), channel_id=1, source_target_pairs={{0,1},{1,2},{2,3},{4,5},{5,6},{6,7},{8,9},{9,10},{10,11},{12,13},{... | collective-permute-start | bytes 3145736 | tf_op jit(solution)/shard_map/while/body/eval_jaxpr/ppermute | solution.py:10
  136.8 1.0 copy-start.1
  137.8 1.7 copy-start.2
  139.5 33.8 %collective-permute-start.1 = (bf16[256,2048]{1,0:T(8,128)(2,1)S(1)}, bf16[256,2048]{1,0:T(8,128)(2,1)}, u32[]{:S(2)}, u32[]{:S(2)}) collective-permute-start(bf16[256,2048]{1,0:T(8,128)(2,1)S(1)} %get-tuple-element.526), channel_id=1, source_target_pairs={{1,0},{2,1},{3,2},{5,4},{6,5},{7,6},{9,8},{10,9},{11,10},{13,12},{... | collective-permute-start | bytes 3145736 | tf_op jit(solution)/shard_map/while/body/eval_jaxpr/ppermute | solution.py:10
  173.3 24.2 %collective-permute-start.1 = (bf16[256,2048]{1,0:T(8,128)(2,1)S(1)}, bf16[256,2048]{1,0:T(8,128)(2,1)}, u32[]{:S(2)}, u32[]{:S(2)}) collective-permute-start(bf16[256,2048]{1,0:T(8,128)(2,1)S(1)} %get-tuple-element.526), channel_id=1, source_target_pairs={{1,0},{2,1},{3,2},{5,4},{6,5},{7,6},{9,8},{10,9},{11,10},{13,12},{... | collective-permute-start | bytes 3145736 | tf_op jit(solution)/shard_map/while/body/eval_jaxpr/ppermute | solution.py:10
  197.5 32.6 %collective-permute-start.1 = (bf16[256,2048]{1,0:T(8,128)(2,1)S(1)}, bf16[256,2048]{1,0:T(8,128)(2,1)}, u32[]{:S(2)}, u32[]{:S(2)}) collective-permute-start(bf16[256,2048]{1,0:T(8,128)(2,1)S(1)} %get-tuple-element.526), channel_id=1, source_target_pairs={{1,0},{2,1},{3,2},{5,4},{6,5},{7,6},{9,8},{10,9},{11,10},{13,12},{... | collective-permute-start | bytes 3145736 | tf_op jit(solution)/shard_map/while/body/eval_jaxpr/ppermute | solution.py:10
  230.1 45.4 %collective-permute-start.1 = (bf16[256,2048]{1,0:T(8,128)(2,1)S(1)}, bf16[256,2048]{1,0:T(8,128)(2,1)}, u32[]{:S(2)}, u32[]{:S(2)}) collective-permute-start(bf16[256,2048]{1,0:T(8,128)(2,1)S(1)} %get-tuple-element.526), channel_id=1, source_target_pairs={{1,0},{2,1},{3,2},{5,4},{6,5},{7,6},{9,8},{10,9},{11,10},{13,12},{... | collective-permute-start | bytes 3145736 | tf_op jit(solution)/shard_map/while/body/eval_jaxpr/ppermute | solution.py:10
  275.5 6.2 %copy-start.6 = (bf16[2048,2048]{1,0:T(8,128)(2,1)S(1)}, bf16[2048,2048]{1,0:T(8,128)(2,1)}, u32[]{:S(2)}) copy-start(bf16[2048,2048]{1,0:T(8,128)(2,1)} %get-tuple-element.351) | copy-start | bytes 25165828 | tf_op jit(solution)/shard_map/while/body/eval_jaxpr/cond
  281.7 2.4 copy-start.3
  286.2 21.3 %copy-start.4 = (f32[1,256,2048]{2,1,0:T(8,128)S(1)}, f32[1,256,2048]{2,1,0:T(8,128)}, u32[]{:S(2)}) copy-start(f32[1,256,2048]{2,1,0:T(8,128)} %get-tuple-element.367) | copy-start | bytes 6291460
  309.2 2.9 copy-start.5
Sparse Core Ops, SparseCore 0:
  312.2 52.3 all-gather.2
